TPU v7x, 32 devices: a whole 2x2x4 slice. The times are simulated.
32 devices in a mesh: fits: 2 (over y), tm: 4 (over z), space: 4 (over x, core).
Axes of the slice: x: 2, y: 2, z: 4, core: 2. Of those that a mesh axis runs over, the one named last changes fastest.
Arguments:
- coupling: float32 [16, 4, 384, 384], P(('fits', 'tm'), 'space'), parts along dimension 0, may hold values from -0.034701105 to 1.0347011, as said below
- schur_inverse: float32 [16, 4, 384, 384], P(('fits', 'tm'), 'space'), parts along dimension 0, may hold values from -0.052051657 to 1.0720517, as said below
- entry_rows: int32 [16, 4, 2048], P(('fits', 'tm'), 'space'), parts along dimension 0, may hold values from 0 to 383
- entry_shift: int32 [16, 4, 2048], P(('fits', 'tm'), 'space'), parts along dimension 0, may hold values from -3 to 3
- entry_hyper: int32 [16, 4, 2048], P(('fits', 'tm'), 'space'), parts along dimension 0, may hold values from 0 to 3
- entry_values: float32 [16, 4, 2048], P(('fits', 'tm'), 'space'), parts along dimension 0, may hold values from -0.3125 to 0.3125
Outputs:
- marginal_cov: float32 [16, 4, 384, 384], P(('fits', 'tm'), 'space'), parts along dimension 0
- gradient: float32 [8], P('fits'), parts along dimension 0
There are 2 independent parts, one for each index of `fits`. A program takes and returns all parts, laid end to end along the dimension named above; each array names one. Nothing has to cross between parts.
Inputs may be any that keep to these rules, and one draw needn't show every extreme that they name: Every block of coupling has entries within the stated range. Every block of schur_inverse is symmetric positive definite.
All inputs are finite; a program needn't handle non-finite values.
Results may differ from a plain program's by a relative error of at most 0.0001.
Values sent between devices are 32-bit elements; how exact they have to be, the bound alone decides.
A program may use at most 128 MiB of HBM per device.

v0:
```python
import jax
import jax.numpy as jnp
from jax import lax
from jax.sharding import PartitionSpec as P

NHYP = 4


def prefix(shard, axis, combine, identity):
    devices, mine = (lax.axis_size(axis), lax.axis_index(axis))
    everything = jax.tree.map(lambda part: lax.all_gather(part, axis), shard)
    start = jax.tree.map(
        lambda part, zero: jnp.broadcast_to(jnp.asarray(zero, part.dtype), part.shape),
        shard,
        identity,
    )

    def step(k, before):
        at = devices - 1 - k
        reached = at > mine
        new = combine(before, jax.tree.map(lambda part: part[at], everything))
        return jax.tree.map(lambda a, b: jnp.where(reached, a, b), new, before)

    return lax.fori_loop(0, devices, step, start)


def apply_map(coupling, schur_inverse, current):
    product = jnp.einsum("sij,sjk->sik", coupling, current, precision=lax.Precision.HIGHEST)
    return (
        jnp.einsum("sik,slk->sil", product, coupling, precision=lax.Precision.HIGHEST)
        + schur_inverse
    )


def combine_maps(earlier, later):
    joined_g = jnp.einsum("sij,sjk->sik", later[0], earlier[0], precision=lax.Precision.HIGHEST)
    joined_s = apply_map(later[0], later[1], earlier[1])
    return (joined_g, joined_s)


def on_device(coupling, schur_inverse, entry_rows, entry_shift, entry_hyper, entry_values):
    time_count = coupling.shape[0]
    order = coupling.shape[2]
    composite_g = coupling[time_count - 1]
    composite_s = schur_inverse[time_count - 1]
    position = 0
    composite_s = apply_map(coupling[position], schur_inverse[position], composite_s)
    composite_g = jnp.einsum(
        "sij,sjk->sik", coupling[position], composite_g, precision=lax.Precision.HIGHEST
    )
    identity = (
        jnp.broadcast_to(jnp.eye(order, dtype=jnp.float32), composite_g.shape),
        jnp.zeros_like(composite_s),
    )
    scanned = prefix((composite_g, composite_s), "tm", combine_maps, identity)
    boundary = scanned[1]
    results = [None] * time_count
    current = boundary
    for position in range(time_count - 1, -1, -1):
        current = apply_map(coupling[position], schur_inverse[position], current)
        results[position] = current
    marginal_cov = jnp.stack(results, axis=0)
    columns = jnp.mod(entry_rows + entry_shift, order)
    flat_index = entry_rows * order + columns
    flattened = marginal_cov.reshape(time_count, coupling.shape[1], order * order)
    picked = jnp.take_along_axis(flattened, flat_index, axis=2)
    one_hot = (entry_hyper[..., None] == jnp.arange(NHYP, dtype=jnp.int32)).astype(jnp.float32)
    local_terms = -0.5 * jnp.sum((entry_values * picked)[..., None] * one_hot, axis=(0, 1, 2))
    gradient = lax.psum(local_terms, ("tm", "space"))
    return (marginal_cov, gradient)


def solution(mesh):
    in_specs = (
        P(("fits", "tm"), "space", None, None),
        P(("fits", "tm"), "space", None, None),
        P(("fits", "tm"), "space", None),
        P(("fits", "tm"), "space", None),
        P(("fits", "tm"), "space", None),
        P(("fits", "tm"), "space", None),
    )
    out_specs = (P(("fits", "tm"), "space", None, None), P("fits"))
    return jax.shard_map(
        on_device, mesh=mesh, in_specs=in_specs, out_specs=out_specs, check_vma=False
    )
```

profile of v0, /device:TPU:0, one launch (start us, length us, event | category | flops | bytes accessed | tf_op | source)
XLA Modules:
  0.0 225.0 jit_solution(2873054929532404826)
XLA Ops:
  7.2 0.0 copy-start
  7.2 0.0 all-gather.7.cloned.1.call-start
  7.2 2.6 %fusion.16 = f32[384,384]{1,0:T(8,128)S(1)} fusion(f32[2,1,384,384]{3,2,1,0:T(8,128)} %param.9, f32[2,1,384,384]{3,2,1,0:T(8,128)} %param.8), kind=kOutput, calls=%fused_computation.23 | convolution fusion | flops 679477248 | bytes 1769472 | tf_op jit(solution)/shard_map/sij,sjk->sik/dot_general | solution.py:28
  9.8 0.0 copy-done
  9.8 3.1 %convolution_add_fusion.3 = f32[384,384]{1,0:T(8,128)} fusion(f32[384,384]{1,0:T(8,128)S(1)} %fusion.16, f32[2,1,384,384]{3,2,1,0:T(8,128)} %param.9, f32[2,1,384,384]{3,2,1,0:T(8,128)S(1)} %copy-done), kind=kOutput, calls=%fused_computation.18 | convolution fusion | flops 679624704 | bytes 2359296 | tf_op jit(solution)/shard_map/sik,slk->sil/dot_general | solution.py:30
  13.0 0.0 all-gather.7.cloned.1.call-update
  13.0 0.0 copy-start.5
  13.0 0.0 copy-start.6
  13.0 0.0 copy-start.7
  13.0 0.0 all-gather.5.cloned.1.call-start
  13.1 2.1 fusion.20
  15.2 0.0 all-gather.5.cloned.1.call-update
  15.2 0.0 copy-done.5
  15.2 0.6 copy.23
  15.8 0.0 copy-done.6
  15.8 0.0 copy-done.7
  15.8 0.7 bitcast_or_fusion
  16.5 49.3 %all-gather.7.cloned.1.call-done = f32[1536,384]{1,0:T(8,128)} async-done(((f32[384,384]{1,0:T(8,128)}), f32[1536,384]{1,0:T(8,128)}) %all-gather.7.cloned.1.call-update) | async-done | bytes 2359312 | tf_op jit(solution)/shard_map/all_gather | solution.py:11
  65.9 50.9 %all-gather.5.cloned.1.call-done = f32[1536,384]{1,0:T(8,128)} async-done(((f32[384,384]{1,0:T(8,128)}), f32[1536,384]{1,0:T(8,128)}) %all-gather.5.cloned.1.call-update) | async-done | bytes 2359312 | tf_op jit(solution)/shard_map/all_gather | solution.py:11
  116.8 19.9 %while.16 = (s32[]{:T(128)}, f32[1,384,384]{2,1,0:T(8,128)S(1)}, s32[]{:T(128)}, f32[4,1,384,384]{3,2,1,0:T(8,128)}, f32[4,1,384,384]{3,2,1,0:T(8,128)}, /*index=5*/s32[]{:T(128)}, s32[]{:T(128)}, s32[]{:T(128)}, s32[]{:T(128)}) while((s32[]{:T(128)}, f32[1,384,384]{2,1,0:T(8,128)S(1)}, s32[]{:T(128)}, ...), condition=%wide.region_1.2_spmd.clone, body=%wide.region_0.1_spmd.clone.sunk | while | flops 1359544320 | bytes 4720802 | solution.py:24
  116.8 2.3 %fusion.54 = f32[384,384]{1,0:T(8,128)S(1)} fusion(f32[1,384,384]{2,1,0:T(8,128)S(1)} %get-tuple-element.221, f32[4,1,384,384]{3,2,1,0:T(8,128)} %get-tuple-element.232, s32[]{:T(128)S(6)} %select_n.74, pred[]{:T(512)S(6)} %compare.3), kind=kOutput, calls=%fused_computation.4.clone.1 | convolution fusion | flops 679624704 | bytes 1769477 | tf_op jit(solution)/shard_map/while/body/eval_jaxpr/sij,sjk->sik/dot_general | solution.py:28
  119.1 2.6 %fusion.55 = f32[1,384,384]{2,1,0:T(8,128)S(1)} fusion(f32[384,384]{1,0:T(8,128)S(1)} %fusion.54, f32[4,1,384,384]{3,2,1,0:T(8,128)} %get-tuple-element.233, s32[]{:T(128)S(6)} %select_n.74, f32[1,384,384]{2,1,0:T(8,128)S(1)} %get-tuple-element.221, f32[4,1,384,384]{3,2,1,0:T(8,128)} %get-tuple-element.232, pred[]{:T(512)S(6)} %compare.3, pred[]{:T(512)S(6)} %gt.12), kind=kOutput, calls=%fused_computation.3.clone.1 | convolution fusion | flops 679919616 | bytes 2951168 | tf_op jit(solution)/shard_map/while/body/eval_jaxpr/sik,slk->sil/dot_general | solution.py:30
  121.8 2.3 %fusion.54 = f32[384,384]{1,0:T(8,128)S(1)} fusion(f32[1,384,384]{2,1,0:T(8,128)S(1)} %get-tuple-element.221, f32[4,1,384,384]{3,2,1,0:T(8,128)} %get-tuple-element.232, s32[]{:T(128)S(6)} %select_n.74, pred[]{:T(512)S(6)} %compare.3), kind=kOutput, calls=%fused_computation.4.clone.1 | convolution fusion | flops 679624704 | bytes 1769477 | tf_op jit(solution)/shard_map/while/body/eval_jaxpr/sij,sjk->sik/dot_general | solution.py:28
  124.1 2.6 %fusion.55 = f32[1,384,384]{2,1,0:T(8,128)S(1)} fusion(f32[384,384]{1,0:T(8,128)S(1)} %fusion.54, f32[4,1,384,384]{3,2,1,0:T(8,128)} %get-tuple-element.233, s32[]{:T(128)S(6)} %select_n.74, f32[1,384,384]{2,1,0:T(8,128)S(1)} %get-tuple-element.221, f32[4,1,384,384]{3,2,1,0:T(8,128)} %get-tuple-element.232, pred[]{:T(512)S(6)} %compare.3, pred[]{:T(512)S(6)} %gt.12), kind=kOutput, calls=%fused_computation.3.clone.1 | convolution fusion | flops 679919616 | bytes 2951168 | tf_op jit(solution)/shard_map/while/body/eval_jaxpr/sik,slk->sil/dot_general | solution.py:30
  126.7 2.3 %fusion.54 = f32[384,384]{1,0:T(8,128)S(1)} fusion(f32[1,384,384]{2,1,0:T(8,128)S(1)} %get-tuple-element.221, f32[4,1,384,384]{3,2,1,0:T(8,128)} %get-tuple-element.232, s32[]{:T(128)S(6)} %select_n.74, pred[]{:T(512)S(6)} %compare.3), kind=kOutput, calls=%fused_computation.4.clone.1 | convolution fusion | flops 679624704 | bytes 1769477 | tf_op jit(solution)/shard_map/while/body/eval_jaxpr/sij,sjk->sik/dot_general | solution.py:28
  129.1 2.6 %fusion.55 = f32[1,384,384]{2,1,0:T(8,128)S(1)} fusion(f32[384,384]{1,0:T(8,128)S(1)} %fusion.54, f32[4,1,384,384]{3,2,1,0:T(8,128)} %get-tuple-element.233, s32[]{:T(128)S(6)} %select_n.74, f32[1,384,384]{2,1,0:T(8,128)S(1)} %get-tuple-element.221, f32[4,1,384,384]{3,2,1,0:T(8,128)} %get-tuple-element.232, pred[]{:T(512)S(6)} %compare.3, pred[]{:T(512)S(6)} %gt.12), kind=kOutput, calls=%fused_computation.3.clone.1 | convolution fusion | flops 679919616 | bytes 2951168 | tf_op jit(solution)/shard_map/while/body/eval_jaxpr/sik,slk->sil/dot_general | solution.py:30
  131.7 2.3 %fusion.54 = f32[384,384]{1,0:T(8,128)S(1)} fusion(f32[1,384,384]{2,1,0:T(8,128)S(1)} %get-tuple-element.221, f32[4,1,384,384]{3,2,1,0:T(8,128)} %get-tuple-element.232, s32[]{:T(128)S(6)} %select_n.74, pred[]{:T(512)S(6)} %compare.3), kind=kOutput, calls=%fused_computation.4.clone.1 | convolution fusion | flops 679624704 | bytes 1769477 | tf_op jit(solution)/shard_map/while/body/eval_jaxpr/sij,sjk->sik/dot_general | solution.py:28
  134.1 2.6 %fusion.55 = f32[1,384,384]{2,1,0:T(8,128)S(1)} fusion(f32[384,384]{1,0:T(8,128)S(1)} %fusion.54, f32[4,1,384,384]{3,2,1,0:T(8,128)} %get-tuple-element.233, s32[]{:T(128)S(6)} %select_n.74, f32[1,384,384]{2,1,0:T(8,128)S(1)} %get-tuple-element.221, f32[4,1,384,384]{3,2,1,0:T(8,128)} %get-tuple-element.232, pred[]{:T(512)S(6)} %compare.3, pred[]{:T(512)S(6)} %gt.12), kind=kOutput, calls=%fused_computation.3.clone.1 | convolution fusion | flops 679919616 | bytes 2951168 | tf_op jit(solution)/shard_map/while/body/eval_jaxpr/sik,slk->sil/dot_general | solution.py:30
  136.7 0.0 copy-start.1
  136.7 2.0 fusion.14
  138.8 0.0 copy-done.1
  138.8 2.0 convolution_add_fusion.2
  140.8 2.9 %fusion.23 = f32[384,384]{1,0:T(8,128)} fusion(f32[384,384]{1,0:T(8,128)S(1)} %convolution_add_fusion.2, f32[2,1,384,384]{3,2,1,0:T(8,128)S(1)} %copy-done), kind=kOutput, calls=%fused_computation.30 | convolution fusion | flops 679477248 | bytes 1769472 | tf_op jit(solution)/shard_map/sij,sjk->sik/dot_general | solution.py:28
  143.7 1.4 stack.19
  145.1 3.1 %convolution_add_fusion.1 = f32[384,384]{1,0:T(8,128)S(1)} fusion(f32[384,384]{1,0:T(8,128)} %fusion.23, f32[2,1,384,384]{3,2,1,0:T(8,128)S(1)} %copy-done.1, f32[2,1,384,384]{3,2,1,0:T(8,128)S(1)} %copy-done), kind=kOutput, calls=%fused_computation.16 | convolution fusion | flops 679624704 | bytes 2359296 | tf_op jit(solution)/shard_map/sik,slk->sil/dot_general | solution.py:30
  148.2 0.0 copy-start.2
  148.2 0.6 stack.18
  148.8 0.5 copy-done.2
  149.2 1.1 maximum_bitcast_fusion
  150.4 0.0 copy-start.4
  150.4 0.0 copy-start.8
  150.4 0.0 copy-start.3
  150.4 34.9 %gather_fusion = f32[4096]{0:T(1024)S(1)} fusion(f32[2,147456]{1,0:T(2,128)S(1)} %maximum_bitcast_fusion, s32[4096]{0:T(1024)S(1)} %bitcast.81), kind=kCustom, calls=%fused_computation | custom fusion | bytes 65536 | tf_op jit(solution)/shard_map/jit(take_along_axis)/gather | solution.py:66
  185.3 0.0 copy-done.4
  185.3 0.0 copy-done.8
  185.4 0.1 select_reduce_fusion
  185.5 31.6 %psum.7 = f32[4]{0:T(128)} all-reduce(f32[4]{0:T(128)S(1)} %broadcast_multiply_fusion), channel_id=1, replica_groups=mesh['fits'=2,'tm'=4,'space'=4] {'tm','space'}, use_global_device_ids=true, to_apply=%region_3.4 | all-reduce | flops 4 | bytes 32 | tf_op jit(solution)/shard_map/psum | solution.py:69
  217.1 1.1 pad_maximum_fusion
  (5 shorter events, 0.1 us)
Async XLA Ops:
  7.2 2.7 %copy-start = (f32[2,1,384,384]{3,2,1,0:T(8,128)S(1)}, f32[2,1,384,384]{3,2,1,0:T(8,128)}, u32[]{:S(2)}) copy-start(f32[2,1,384,384]{3,2,1,0:T(8,128)} %param.8) | copy-start | bytes 3538948
  7.2 58.7 %all-gather.7.cloned.1.call-start = ((), (), s32[]{:S(2)}) async-start(), calls=%async_computation.1 | async-start | bytes 2949120 | tf_op jit(solution)/shard_map/all_gather | solution.py:11
  13.0 2.2 copy-start.5
  13.0 2.8 %copy-start.6 = (s32[2,1,2048]{2,1,0:T(1,128)S(1)}, s32[2,1,2048]{2,1,0:T(1,128)}, u32[]{:S(2)}) copy-start(s32[2,1,2048]{2,1,0:T(1,128)} %param.10) | copy-start | bytes 49156
  13.0 2.8 %copy-start.7 = (s32[2,1,2048]{2,1,0:T(1,128)S(1)}, s32[2,1,2048]{2,1,0:T(1,128)}, u32[]{:S(2)}) copy-start(s32[2,1,2048]{2,1,0:T(1,128)} %param.11) | copy-start | bytes 49156
  13.0 103.7 %all-gather.5.cloned.1.call-start = ((), (), s32[]{:S(2)}) async-start(), calls=%async_computation | async-start | bytes 2949120 | tf_op jit(solution)/shard_map/all_gather | solution.py:11
  136.7 2.1 copy-start.1
  148.2 1.1 copy-start.2
  150.4 35.0 %copy-start.4 = (s32[2,1,2048]{2,1,0:T(1,128)S(1)}, s32[2,1,2048]{2,1,0:T(1,128)}, u32[]{:S(2)}) copy-start(s32[2,1,2048]{2,1,0:T(1,128)} %get-tuple-element.179) | copy-start | bytes 49156
  150.4 35.0 %copy-start.8 = (f32[2,1,2048]{2,1,0:T(1,128)S(1)}, f32[2,1,2048]{2,1,0:T(1,128)}, u32[]{:S(2)}) copy-start(f32[2,1,2048]{2,1,0:T(1,128)} %param.13) | copy-start | bytes 49156
  150.4 35.0 %copy-start.3 = (s32[2,1,2048]{2,0,1:T(2,128)S(1)}, s32[2,1,2048]{2,0,1:T(2,128)}, u32[]{:S(2)}) copy-start(s32[2,1,2048]{2,0,1:T(2,128)} %copy.23) | copy-start | bytes 49156
Sparse Core Ops, SparseCore 0:
  13.1 52.6 all-gather.6
  68.0 48.7 all-gather.4
where the time goes:
time: 226 us; the launch traced here: 225 us
  waiting for transfers between devices  100 us (44%)
  local copies, waits for them, and re-layouts  38 us (17%)
  matrix products  37.6 us (17%)
  blocking collectives  31.6 us (14%)
  between operations  14.3 us (6%)
  other arithmetic  3.1 us (1%)
    all_gather x2, waiting for transfers between devices, prefix(): everything = jax.tree.map(lambda part: lax.all_gather(part, axis), shard)  100 us
    gather x1, local copies, waits for them, and re-layouts, on_device(): picked = jnp.take_along_axis(flattened, flat_index, axis=2)  34.9 us
    psum x1, blocking collectives, on_device(): gradient = lax.psum(local_terms, ('tm', 'space'))  31.6 us
    dot_general x7, matrix products, apply_map(): jnp.einsum('sik,slk->sil', product, coupling, precision=lax.Precision.HIG...  18.8 us
    dot_general x7, matrix products, apply_map(): jnp.einsum('sij,sjk->sik', coupling, current, precision=lax.Precision.HIG...  16.8 us
  transfers between devices with their start and end apart: 2, of which 2 were waited for; matrix products, arithmetic and copies ran while one was open for 2% of the time, Pallas kernels for 0%

commit v1 on v0

v1 whole, which is shorter than its diff:
```python
import functools

import jax
import jax.numpy as jnp
from jax import lax
from jax.experimental import pallas as pl
from jax.experimental.pallas import tpu as pltpu
from jax.sharding import PartitionSpec as P

NHYP = 4
REACH = 3
TILE = 128
MESH = pl.DeviceIdType.MESH
F32 = jnp.float32
BF16 = jnp.bfloat16
NN = (((1,), (0,)), ((), ()))
NT = (((1,), (1,)), ((), ()))


def split(x):
    hi = x.astype(BF16)
    return hi, (x - hi.astype(F32)).astype(BF16)


def product(a, b, dims):
    def one(x, y):
        return lax.dot_general(x, y, dims, preferred_element_type=F32)

    return one(a[0], b[0]) + (one(a[0], b[1]) + one(a[1], b[0]))


def kernel(
    coupling_hbm,
    schur_hbm,
    rows_ref,
    shift_ref,
    hyper_ref,
    values_ref,
    out_hbm,
    grad_ref,
    g_in,
    s_in,
    result,
    g_hi,
    g_lo,
    c_hi,
    c_lo,
    b_hi,
    b_lo,
    q_hi,
    q_lo,
    outgoing,
    incoming,
    weights,
    partials,
    load_sem,
    store_sem,
    send_sem,
    recv_sem,
    turn_sem,
    part_send,
    part_recv,
):
    steps = g_in.shape[0]
    order = g_in.shape[1]
    blocks = order // TILE
    devices, spaces = lax.axis_size("tm"), lax.axis_size("space")
    me, mine = lax.axis_index("tm"), lax.axis_index("space")
    group = devices * spaces
    rank = me * spaces + mine
    is_last = me == devices - 1
    staggered = spaces % 2 == 0 and spaces > 1

    def peer(k):
        other = lax.rem(rank + k, group)
        return other, {"tm": other // spaces, "space": lax.rem(other, spaces)}

    loads = []
    for p in range(steps - 1, -1, -1):
        for which, (source, target) in enumerate(((coupling_hbm, g_in), (schur_hbm, s_in))):
            copy = pltpu.make_async_copy(source.at[p, 0], target.at[p], load_sem.at[which, p])
            copy.start()
            loads.append(copy)

    barrier = pltpu.get_barrier_semaphore()

    def greet(k, carry):
        _, where = peer(k)
        pl.semaphore_signal(barrier, inc=1, device_id=where, device_id_type=MESH)
        return carry

    lax.fori_loop(1, group, greet, 0)

    for copy in loads:
        copy.wait()

    def band(i):
        return slice(i * TILE, (i + 1) * TILE)

    for p in range(steps):
        g_hi[p], g_lo[p] = split(g_in[p])

    def set_current(x):
        b_hi[...], b_lo[...] = split(x)

    def first_half(gh, gl, i):
        part = product((b_hi[band(i), :], b_lo[band(i), :]), (gh[...], gl[...]), NT)
        q_hi[band(i), :], q_lo[band(i), :] = split(part)

    def second_half(gh, gl, add, i):
        right = slice(i * TILE, order)
        part = product(
            (gh[band(i), :], gl[band(i), :]), (q_hi[:, right], q_lo[:, right]), NN
        )
        return part + add[band(i), right]

    def mirror(target):
        for i in range(blocks):
            for j in range(i + 1, blocks):
                target[band(j), band(i)] = target[band(i), band(j)].T

    def hop(i):
        region = (band(i), slice(i * TILE, order))
        return pltpu.make_async_remote_copy(
            src_ref=outgoing.at[region],
            dst_ref=incoming.at[region],
            send_sem=send_sem.at[i],
            recv_sem=recv_sem.at[i],
            device_id={"tm": me - 1},
            device_id_type=MESH,
        )

    set_current(s_in[steps - 1])
    result[steps - 1] = s_in[steps - 1]
    for p in range(steps - 2, -1, -1):
        for i in range(blocks):
            first_half(g_hi.at[p], g_lo.at[p], i)
        for i in range(blocks):
            result[p, band(i), i * TILE :] = second_half(g_hi.at[p], g_lo.at[p], s_in.at[p], i)
        if p > 0:
            mirror(result.at[p])
            set_current(result[p])

    pl.semaphore_wait(barrier, group - 1)

    if devices > 1:

        @pl.when(is_last)
        def _():
            for i in range(blocks):
                right = slice(i * TILE, order)
                outgoing[band(i), right] = result[0, band(i), right]
            if staggered:

                @pl.when(lax.rem(mine, 2) == 1)
                def _():
                    pl.semaphore_wait(turn_sem, 1)

            for i in range(blocks):
                hop(i).start()

        @pl.when(jnp.logical_not(is_last))
        def _():
            if steps > 1:
                joined = product(
                    (g_hi[0], g_lo[0]), (g_hi[1], g_lo[1]), NN
                )
                c_hi[...], c_lo[...] = split(joined)
                for p in range(2, steps):
                    joined = product((c_hi[...], c_lo[...]), (g_hi[p], g_lo[p]), NN)
                    c_hi[...], c_lo[...] = split(joined)
            else:
                c_hi[...], c_lo[...] = g_hi[0], g_lo[0]

    codes = NHYP * (2 * REACH + 1)
    padded = weights.shape[1]
    count = rows_ref.shape[2]
    for p in range(steps):
        code = (shift_ref[p] + REACH) * NHYP + hyper_ref[p]
        chosen = lax.broadcasted_iota(jnp.int32, (padded, count), 0) == code
        value = values_ref[p]
        parts = []
        rest = value
        for _ in range(3):
            piece = rest.astype(BF16).astype(F32)
            parts.append(jnp.where(chosen, piece, 0.0).astype(BF16))
            rest = rest - piece
        spread = jnp.concatenate(parts, axis=0)
        placed = lax.broadcasted_iota(jnp.int32, (order, count), 0) == rows_ref[p]
        onehot = jnp.where(placed, 1.0, 0.0).astype(BF16)
        sums = lax.dot_general(spread, onehot, NT, preferred_element_type=F32)
        weights[p] = sums[:padded] + sums[padded : 2 * padded] + sums[2 * padded :]

    if devices > 1:
        if staggered:

            @pl.when(jnp.logical_and(is_last, lax.rem(mine, 2) == 0))
            def _():
                for i in range(blocks):
                    hop(i).wait_send()
                pl.semaphore_signal(
                    turn_sem, inc=1, device_id={"space": mine + 1}, device_id_type=MESH
                )

            @pl.when(jnp.logical_and(is_last, lax.rem(mine, 2) == 1))
            def _():
                for i in range(blocks):
                    hop(i).wait_send()
        else:

            @pl.when(is_last)
            def _():
                for i in range(blocks):
                    hop(i).wait_send()

        @pl.when(jnp.logical_not(is_last))
        def _():
            for i in range(blocks):
                hop(i).wait_recv()
                for j in range(i, blocks):
                    block = incoming[band(i), band(j)]
                    b_hi[band(i), band(j)], b_lo[band(i), band(j)] = split(block)
                    if j > i:
                        b_hi[band(j), band(i)], b_lo[band(j), band(i)] = split(block.T)
                first_half(c_hi, c_lo, i)
            for i in range(blocks):
                right = slice(i * TILE, order)
                fresh = second_half(c_hi, c_lo, result.at[0], i)
                result[0, band(i), right] = fresh

                @pl.when(me > 0)
                def _():
                    outgoing[band(i), right] = fresh
                    hop(i).start()

            for p in range(steps - 1, 0, -1):
                for i in range(blocks):
                    first_half(g_hi.at[p], g_lo.at[p], i)
                for i in range(blocks):
                    result[p, band(i), i * TILE :] = second_half(
                        g_hi.at[p], g_lo.at[p], s_in.at[p], i
                    )
                mirror(result.at[p])
                if p > 1:
                    set_current(result[p])

    if steps > 1 or devices > 1:
        mirror(result.at[0])

    stores = []
    for p in range(steps):
        copy = pltpu.make_async_copy(result.at[p], out_hbm.at[p, 0], store_sem.at[p])
        copy.start()
        stores.append(copy)

    def diagonals(p):
        pieces = []
        for b in range(blocks):
            above = (b * TILE - 8) % order
            below = (b + 1) * TILE % order
            strips = (
                (result[p, above : above + 8, band(b)], -8, 8),
                (result[p, band(b), band(b)], 0, TILE),
                (result[p, below : below + 8, band(b)], TILE, 8),
            )
            lines = [jnp.zeros((1, TILE), F32) for _ in range(2 * REACH + 1)]
            for block, base, height in strips:
                row = lax.broadcasted_iota(jnp.int32, (height, TILE), 0) + base
                offset = row - lax.broadcasted_iota(jnp.int32, (height, TILE), 1)
                for d in range(2 * REACH + 1):
                    lines[d] = lines[d] + jnp.sum(
                        jnp.where(offset == d - REACH, block, 0.0), axis=0, keepdims=True
                    )
            pieces.append(lines)
        return pieces

    total = jnp.zeros((8, TILE), F32)
    group_of = lax.broadcasted_iota(jnp.int32, (padded, TILE), 0) // NHYP
    for p in range(steps):
        for b, lines in enumerate(diagonals(p)):
            matched = jnp.zeros((padded, TILE), F32)
            for d in range(2 * REACH + 1):
                matched = jnp.where(group_of == d, lines[d], matched)
            terms = matched * weights[p, :, band(b)]
            for k in range(padded // 8):
                total = total + terms[8 * k : 8 * (k + 1)]
    partials[rank] = total

    def exchange(k):
        other, where = peer(k)
        return pltpu.make_async_remote_copy(
            src_ref=partials.at[rank],
            dst_ref=partials.at[rank],
            send_sem=part_send.at[k],
            recv_sem=part_recv.at[rank],
            device_id=where,
            device_id_type=MESH,
        )

    def start_exchange(k, carry):
        exchange(k).start()
        return carry

    lax.fori_loop(1, group, start_exchange, 0)

    def take(k, carry):
        other, where = peer(k)
        pltpu.make_async_remote_copy(
            src_ref=partials.at[other],
            dst_ref=partials.at[other],
            send_sem=part_send.at[k],
            recv_sem=part_recv.at[other],
            device_id=where,
            device_id_type=MESH,
        ).wait_recv()
        return carry

    lax.fori_loop(1, group, take, 0)
    everything = jnp.sum(partials[...], axis=0)
    everything = everything[:NHYP] + everything[NHYP : 2 * NHYP]
    for k in range(NHYP):
        grad_ref[k] = -0.5 * jnp.sum(everything[k : k + 1])

    def finish_exchange(k, carry):
        exchange(k).wait_send()
        return carry

    lax.fori_loop(1, group, finish_exchange, 0)
    if devices > 1:

        @pl.when(jnp.logical_and(me > 0, jnp.logical_not(is_last)))
        def _():
            for i in range(blocks):
                hop(i).wait_send()

    for copy in stores:
        copy.wait()


def on_device(group, coupling, schur_inverse, entry_rows, entry_shift, entry_hyper, entry_values):
    steps, _, order, _ = coupling.shape
    blocks = order // TILE
    whole = pl.BlockSpec(memory_space=pltpu.VMEM)
    apart = pl.BlockSpec(memory_space=pl.ANY)
    padded = 32
    return pl.pallas_call(
        kernel,
        out_shape=(
            jax.ShapeDtypeStruct(coupling.shape, F32),
            jax.ShapeDtypeStruct((NHYP,), F32),
        ),
        in_specs=[apart, apart, whole, whole, whole, whole],
        out_specs=(apart, pl.BlockSpec(memory_space=pltpu.SMEM)),
        scratch_shapes=[
            pltpu.VMEM((steps, order, order), F32),
            pltpu.VMEM((steps, order, order), F32),
            pltpu.VMEM((steps, order, order), F32),
            pltpu.VMEM((steps, order, order), BF16),
            pltpu.VMEM((steps, order, order), BF16),
            pltpu.VMEM((order, order), BF16),
            pltpu.VMEM((order, order), BF16),
            pltpu.VMEM((order, order), BF16),
            pltpu.VMEM((order, order), BF16),
            pltpu.VMEM((order, order), BF16),
            pltpu.VMEM((order, order), BF16),
            pltpu.VMEM((order, order), F32),
            pltpu.VMEM((order, order), F32),
            pltpu.VMEM((steps, padded, order), F32),
            pltpu.VMEM((group, 8, TILE), F32),
            pltpu.SemaphoreType.DMA((2, steps)),
            pltpu.SemaphoreType.DMA((steps,)),
            pltpu.SemaphoreType.DMA((blocks,)),
            pltpu.SemaphoreType.DMA((blocks,)),
            pltpu.SemaphoreType.REGULAR,
            pltpu.SemaphoreType.DMA((group,)),
            pltpu.SemaphoreType.DMA((group,)),
        ],
        compiler_params=pltpu.CompilerParams(collective_id=0, has_side_effects=True),
    )(coupling, schur_inverse, entry_rows, entry_shift, entry_hyper, entry_values)


def solution(mesh):
    group = mesh.shape["tm"] * mesh.shape["space"]
    in_specs = (
        P(("fits", "tm"), "space", None, None),
        P(("fits", "tm"), "space", None, None),
        P(("fits", "tm"), "space", None),
        P(("fits", "tm"), "space", None),
        P(("fits", "tm"), "space", None),
        P(("fits", "tm"), "space", None),
    )
    out_specs = (P(("fits", "tm"), "space", None, None), P("fits"))
    return jax.shard_map(
        functools.partial(on_device, group),
        mesh=mesh,
        in_specs=in_specs,
        out_specs=out_specs,
        check_vma=False,
    )
```

time: 226 us -> 45.3 us (0.20)
  waiting for transfers between devices: 100 us -> 0 us
  Pallas kernels: 0 us -> 41.5 us
  matrix products: 37.6 us -> 0 us
  local copies, waits for them, and re-layouts: 38 us -> 2.88 us
  blocking collectives: 31.6 us -> 0 us
  between operations: 14.3 us -> 0.65 us
  other arithmetic: 3.1 us -> 0 us
    all_gather x2 -> x0, waiting for transfers between devices: 100 us -> none  [prefix(): everything = jax.tree.map(lambda part: lax.all_gather(part, axis), shard)]
    pallas_call x0 -> x1, Pallas kernels: none -> 41.5 us  [on_device(): pl.pallas_call(kernel, out_shape=(jax.ShapeDtypeStruct(coupling.shape, F3...]
    dot_general x15 -> x0, matrix products: 37.6 us -> none  [the longest x7 18.8 us: apply_map(): jnp.einsum('sik,slk->sil', product, coupling, precision=lax.Precision.HIG...]
    gather x1 -> x0, local copies, waits for them, and re-layouts: 34.9 us -> none  [on_device(): picked = jnp.take_along_axis(flattened, flat_index, axis=2)]
    psum x1 -> x0, blocking collectives: 31.6 us -> none  [on_device(): gradient = lax.psum(local_terms, ('tm', 'space'))]
  transfers between devices with their start and end apart: 2 -> 0, of which waited for: 2 -> 0; matrix products, arithmetic and copies ran while one was open for 2% -> 0% of each run, Pallas kernels for 0% -> 0%
where the time goes in v1:
time: 45.3 us; the launch traced here: 45 us
  Pallas kernels  41.5 us (92%)
  local copies, waits for them, and re-layouts  2.88 us (6%)
  between operations  0.65 us (1%)
    pallas_call x1, Pallas kernels, on_device(): pl.pallas_call(kernel, out_shape=(jax.ShapeDtypeStruct(coupling.shape, F3...  41.5 us
    unnamed x4, local copies, waits for them, and re-layouts  2.88 us

profile of v1, /device:TPU:0, one launch (start us, length us, event | category | flops | bytes accessed | tf_op | source)
XLA Modules:
  0.0 45.0 jit_solution(7065881342073688929)
XLA Ops:
  0.6 41.5 %shard_map.77 = (f32[2,1,384,384]{3,2,1,0:T(8,128)}, f32[4]{0:T(128)}) custom-call(f32[2,1,384,384]{3,2,1,0:T(8,128)} %coupling_hbm.1, f32[2,1,384,384]{3,2,1,0:T(8,128)} %schur_hbm.1, s32[2,1,2048]{2,1,0:T(1,128)} %rows_ref.1, s32[2,1,2048]{2,1,0:T(1,128)} %shift_ref.1, s32[2,1,2048]{2,1,0:T(1,128)} %hyper_ref.1, f32[2,1,2048]{2,1,0:T(1,128)} %values_ref.1), custom_call_target="tpu_custom_call" | custom-call | tf_op jit(solution)/shard_map/pallas_call | solution.py:346
  42.1 0.0 copy-start
  42.2 2.4 %copy.10 = f32[2,1,384,384]{3,2,1,0:T(8,128)} copy(f32[2,1,384,384]{3,2,1,0:T(8,128)} %get-tuple-element.4) | data formatting | bytes 2359296
  44.5 0.0 copy-done
  44.5 0.5 %copy.11 = f32[4]{0:T(128)} copy(f32[4]{0:T(128)S(1)} %copy-done) | data formatting | bytes 32
Async XLA Ops:
  42.1 2.4 %copy-start = (f32[4]{0:T(128)S(1)}, f32[4]{0:T(128)}, u32[]{:S(2)}) copy-start(f32[4]{0:T(128)} %get-tuple-element.5) | copy-start | bytes 52

commit v2 on v1

--- a/solution.py
+++ b/solution.py
@@ -13,6 +13,7 @@
 MESH = pl.DeviceIdType.MESH
 F32 = jnp.float32
 BF16 = jnp.bfloat16
+OUT_TYPE = pltpu.VMEM
 NN = (((1,), (0,)), ((), ()))
 NT = (((1,), (1,)), ((), ()))
 
@@ -32,15 +33,18 @@
 def kernel(
     coupling_hbm,
     schur_hbm,
+    rows_hbm,
+    shift_hbm,
+    hyper_hbm,
+    values_hbm,
+    out_ref,
+    grad_ref,
+    g_in,
+    s_in,
     rows_ref,
     shift_ref,
     hyper_ref,
     values_ref,
-    out_hbm,
-    grad_ref,
-    g_in,
-    s_in,
-    result,
     g_hi,
     g_lo,
     c_hi,
@@ -49,12 +53,16 @@
     b_lo,
     q_hi,
     q_lo,
-    outgoing,
-    incoming,
+    out_a,
+    out_b,
+    out_c,
+    in_a,
+    in_b,
+    in_c,
     weights,
     partials,
     load_sem,
-    store_sem,
+    entry_sem,
     send_sem,
     recv_sem,
     turn_sem,
@@ -70,17 +78,39 @@
     rank = me * spaces + mine
     is_last = me == devices - 1
     staggered = spaces % 2 == 0 and spaces > 1
+    goes_first = lax.rem(mine, 2) == 0 if staggered else mine >= 0
 
     def peer(k):
         other = lax.rem(rank + k, group)
         return other, {"tm": other // spaces, "space": lax.rem(other, spaces)}
 
-    loads = []
-    for p in range(steps - 1, -1, -1):
-        for which, (source, target) in enumerate(((coupling_hbm, g_in), (schur_hbm, s_in))):
-            copy = pltpu.make_async_copy(source.at[p, 0], target.at[p], load_sem.at[which, p])
-            copy.start()
-            loads.append(copy)
+    result = out_ref.at[:, 0]
+    sources = (coupling_hbm, schur_hbm)
+    targets = (g_in, s_in)
+
+    def load(which, p):
+        return pltpu.make_async_copy(
+            sources[which].at[p, 0], targets[which].at[p], load_sem.at[which, p]
+        )
+
+    order_of_loads = [(1, steps - 1)]
+    for p in range(steps - 2, -1, -1):
+        order_of_loads += [(0, p), (1, p)]
+    order_of_loads.append((0, steps - 1))
+    for which, p in order_of_loads:
+        load(which, p).start()
+    entries = []
+    for k, (source, target) in enumerate(
+        (
+            (rows_hbm, rows_ref),
+            (shift_hbm, shift_ref),
+            (hyper_hbm, hyper_ref),
+            (values_hbm, values_ref),
+        )
+    ):
+        copy = pltpu.make_async_copy(source, target, entry_sem.at[k])
+        copy.start()
+        entries.append(copy)
 
     barrier = pltpu.get_barrier_semaphore()
 
@@ -91,14 +121,8 @@
 
     lax.fori_loop(1, group, greet, 0)
 
-    for copy in loads:
-        copy.wait()
-
     def band(i):
         return slice(i * TILE, (i + 1) * TILE)
-
-    for p in range(steps):
-        g_hi[p], g_lo[p] = split(g_in[p])
 
     def set_current(x):
         b_hi[...], b_lo[...] = split(x)
@@ -119,58 +143,154 @@
             for j in range(i + 1, blocks):
                 target[band(j), band(i)] = target[band(i), band(j)].T
 
+    chunks = ((out_a, in_a), (out_b, in_b), (out_c, in_c))
+
     def hop(i):
-        region = (band(i), slice(i * TILE, order))
         return pltpu.make_async_remote_copy(
-            src_ref=outgoing.at[region],
-            dst_ref=incoming.at[region],
+            src_ref=chunks[i][0],
+            dst_ref=chunks[i][1],
             send_sem=send_sem.at[i],
             recv_sem=recv_sem.at[i],
             device_id={"tm": me - 1},
             device_id_type=MESH,
         )
 
+    half = TILE // 2
+
+    def places(height=TILE):
+        down = lax.broadcasted_iota(jnp.int32, (height, TILE), 0)
+        return down, lax.broadcasted_iota(jnp.int32, (height, TILE), 1)
+
+    def diagonal_of(x):
+        down, across = places()
+        return jnp.sum(jnp.where(across == down, x, 0.0), axis=0, keepdims=True)
+
+    def pack(i, source):
+        if i == 0:
+            out_a[...] = source[band(0), TILE:]
+        elif i == 1:
+            down, across = places()
+            second = source[band(1), band(1)]
+            out_b[:TILE, :TILE] = jnp.where(across >= down, source[band(0), band(0)], second.T)
+            out_b[:TILE, TILE:] = source[band(1), band(2)]
+            line = jnp.broadcast_to(diagonal_of(second), (8, TILE))
+            out_b[TILE:, :] = jnp.concatenate([line, line], axis=1)
+        else:
+            down, across = places(half)
+            third = source[band(2), band(2)]
+            turned = pltpu.roll(third.T, half, 1)
+            out_c[:half, :] = jnp.where(across >= down, third[:half], turned[half:])
+            out_c[half:, :] = jnp.broadcast_to(diagonal_of(third), (8, TILE))
+
+    def put(i, j, block):
+        b_hi[band(i), band(j)], b_lo[band(i), band(j)] = split(block)
+        if i != j:
+            b_hi[band(j), band(i)], b_lo[band(j), band(i)] = split(block.T)
+
+    def unpack(i):
+        if i == 0:
+            put(0, 1, in_a[:, :TILE])
+            put(0, 2, in_a[:, TILE:])
+        elif i == 1:
+            down, across = places()
+            upper, diagonal = across >= down, across == down
+            shared = in_b[:TILE, :TILE]
+            turned = shared.T
+            put(0, 0, jnp.where(upper, shared, turned))
+            second = jnp.where(upper, turned, shared)
+            put(1, 1, jnp.where(diagonal, in_b[TILE : TILE + 1, :TILE], second))
+            put(1, 2, in_b[:TILE, TILE:])
+        else:
+            top = in_c[:half, :]
+            corner = pltpu.roll(top, half, 1)
+            low, along = places(half)
+            one_side = jnp.concatenate(
+                [
+                    jnp.where(along >= low, top, 0.0),
+                    jnp.where(
+                        jnp.logical_and(along >= half, along < low + half), corner, 0.0
+                    ),
+                ],
+                axis=0,
+            )
+            down, across = places()
+            diagonal = across == down
+            other = jnp.where(diagonal, 0.0, one_side)
+            third = one_side + other.T
+            third = jnp.where(diagonal, in_c[half : half + 1, :], third)
+            put(2, 2, third)
+
+    load(1, steps - 1).wait()
     set_current(s_in[steps - 1])
     result[steps - 1] = s_in[steps - 1]
     for p in range(steps - 2, -1, -1):
+        load(0, p).wait()
+        g_hi[p], g_lo[p] = split(g_in[p])
         for i in range(blocks):
             first_half(g_hi.at[p], g_lo.at[p], i)
+        load(1, p).wait()
         for i in range(blocks):
             result[p, band(i), i * TILE :] = second_half(g_hi.at[p], g_lo.at[p], s_in.at[p], i)
+            if p == 0 and devices > 1:
+                if i == 0:
+                    pl.semaphore_wait(barrier, group - 1)
+
+                @pl.when(is_last)
+                def _():
+                    pack(i, result.at[0])
+
+                @pl.when(jnp.logical_and(is_last, goes_first))
+                def _():
+                    hop(i).start()
         if p > 0:
             mirror(result.at[p])
             set_current(result[p])
-
-    pl.semaphore_wait(barrier, group - 1)
+    if steps == 1 or devices == 1:
+        pl.semaphore_wait(barrier, group - 1)
 
     if devices > 1:
-
-        @pl.when(is_last)
+        if steps == 1:
+
+            @pl.when(is_last)
+            def _():
+                for i in range(blocks):
+                    pack(i, result.at[0])
+
+            @pl.when(jnp.logical_and(is_last, goes_first))
+            def _():
+                for i in range(blocks):
+                    hop(i).start()
+
+        @pl.when(jnp.logical_and(is_last, goes_first))
         def _():
             for i in range(blocks):
-                right = slice(i * TILE, order)
-                outgoing[band(i), right] = result[0, band(i), right]
-            if staggered:
-
-                @pl.when(lax.rem(mine, 2) == 1)
-                def _():
-                    pl.semaphore_wait(turn_sem, 1)
-
-            for i in range(blocks):
-                hop(i).start()
+                if staggered and i == blocks - 1:
+                    pl.semaphore_signal(
+                        turn_sem, inc=1, device_id={"space": mine + 1}, device_id_type=MESH
+                    )
+                hop(i).wait_send()
+
+        if staggered:
+
+            @pl.when(jnp.logical_and(is_last, jnp.logical_not(goes_first)))
+            def _():
+                pl.semaphore_wait(turn_sem, 1)
+                for i in range(blocks):
+                    hop(i).start()
+
+    load(0, steps - 1).wait()
+    g_hi[steps - 1], g_lo[steps - 1] = split(g_in[steps - 1])
+    if devices > 1:
 
         @pl.when(jnp.logical_not(is_last))
         def _():
-            if steps > 1:
-                joined = product(
-                    (g_hi[0], g_lo[0]), (g_hi[1], g_lo[1]), NN
-                )
+            c_hi[...], c_lo[...] = g_hi[0], g_lo[0]
+            for p in range(1, steps):
+                joined = product((c_hi[...], c_lo[...]), (g_hi[p], g_lo[p]), NN)
                 c_hi[...], c_lo[...] = split(joined)
-                for p in range(2, steps):
-                    joined = product((c_hi[...], c_lo[...]), (g_hi[p], g_lo[p]), NN)
-                    c_hi[...], c_lo[...] = split(joined)
-            else:
-                c_hi[...], c_lo[...] = g_hi[0], g_lo[0]
+
+    for copy in entries:
+        copy.wait()
 
     codes = NHYP * (2 * REACH + 1)
     padded = weights.shape[1]
@@ -192,37 +312,16 @@
         weights[p] = sums[:padded] + sums[padded : 2 * padded] + sums[2 * padded :]
 
     if devices > 1:
-        if staggered:
-
-            @pl.when(jnp.logical_and(is_last, lax.rem(mine, 2) == 0))
-            def _():
-                for i in range(blocks):
-                    hop(i).wait_send()
-                pl.semaphore_signal(
-                    turn_sem, inc=1, device_id={"space": mine + 1}, device_id_type=MESH
-                )
-
-            @pl.when(jnp.logical_and(is_last, lax.rem(mine, 2) == 1))
-            def _():
-                for i in range(blocks):
-                    hop(i).wait_send()
-        else:
-
-            @pl.when(is_last)
-            def _():
-                for i in range(blocks):
-                    hop(i).wait_send()
 
         @pl.when(jnp.logical_not(is_last))
         def _():
             for i in range(blocks):
                 hop(i).wait_recv()
-                for j in range(i, blocks):
-                    block = incoming[band(i), band(j)]
-                    b_hi[band(i), band(j)], b_lo[band(i), band(j)] = split(block)
-                    if j > i:
-                        b_hi[band(j), band(i)], b_lo[band(j), band(i)] = split(block.T)
-                first_half(c_hi, c_lo, i)
+                unpack(i)
+                if i == 1:
+                    first_half(c_hi, c_lo, 0)
+                if i > 0:
+                    first_half(c_hi, c_lo, i)
             for i in range(blocks):
                 right = slice(i * TILE, order)
                 fresh = second_half(c_hi, c_lo, result.at[0], i)
@@ -230,7 +329,7 @@
 
                 @pl.when(me > 0)
                 def _():
-                    outgoing[band(i), right] = fresh
+                    pack(i, result.at[0])
                     hop(i).start()
 
             for p in range(steps - 1, 0, -1):
@@ -246,12 +345,6 @@
 
     if steps > 1 or devices > 1:
         mirror(result.at[0])
-
-    stores = []
-    for p in range(steps):
-        copy = pltpu.make_async_copy(result.at[p], out_hbm.at[p, 0], store_sem.at[p])
-        copy.start()
-        stores.append(copy)
 
     def diagonals(p):
         pieces = []
@@ -333,8 +426,12 @@
             for i in range(blocks):
                 hop(i).wait_send()
 
-    for copy in stores:
-        copy.wait()
+        if staggered:
+
+            @pl.when(jnp.logical_and(is_last, jnp.logical_not(goes_first)))
+            def _():
+                for i in range(blocks):
+                    hop(i).wait_send()
 
 
 def on_device(group, coupling, schur_inverse, entry_rows, entry_shift, entry_hyper, entry_values):
@@ -343,18 +440,24 @@
     whole = pl.BlockSpec(memory_space=pltpu.VMEM)
     apart = pl.BlockSpec(memory_space=pl.ANY)
     padded = 32
+    entries = (entry_rows, entry_shift, entry_hyper, entry_values)
+    travelling = [
+        pltpu.VMEM((TILE, 2 * TILE), F32),
+        pltpu.VMEM((TILE + 8, 2 * TILE), F32),
+        pltpu.VMEM((TILE // 2 + 8, TILE), F32),
+    ]
     return pl.pallas_call(
         kernel,
         out_shape=(
-            jax.ShapeDtypeStruct(coupling.shape, F32),
+            OUT_TYPE(coupling.shape, F32),
             jax.ShapeDtypeStruct((NHYP,), F32),
         ),
-        in_specs=[apart, apart, whole, whole, whole, whole],
-        out_specs=(apart, pl.BlockSpec(memory_space=pltpu.SMEM)),
+        in_specs=[apart] * 6,
+        out_specs=(whole, pl.BlockSpec(memory_space=pltpu.SMEM)),
         scratch_shapes=[
             pltpu.VMEM((steps, order, order), F32),
             pltpu.VMEM((steps, order, order), F32),
-            pltpu.VMEM((steps, order, order), F32),
+            *[pltpu.VMEM(x.shape, x.dtype) for x in entries],
             pltpu.VMEM((steps, order, order), BF16),
             pltpu.VMEM((steps, order, order), BF16),
             pltpu.VMEM((order, order), BF16),
@@ -363,12 +466,12 @@
             pltpu.VMEM((order, order), BF16),
             pltpu.VMEM((order, order), BF16),
             pltpu.VMEM((order, order), BF16),
-            pltpu.VMEM((order, order), F32),
-            pltpu.VMEM((order, order), F32),
+            *travelling,
+            *travelling,
             pltpu.VMEM((steps, padded, order), F32),
             pltpu.VMEM((group, 8, TILE), F32),
             pltpu.SemaphoreType.DMA((2, steps)),
-            pltpu.SemaphoreType.DMA((steps,)),
+            pltpu.SemaphoreType.DMA((len(entries),)),
             pltpu.SemaphoreType.DMA((blocks,)),
             pltpu.SemaphoreType.DMA((blocks,)),
             pltpu.SemaphoreType.REGULAR,

time: 45.3 us -> 39.9 us (0.88)
  Pallas kernels: 41.5 us -> 37.6 us
  local copies, waits for them, and re-layouts: 2.88 us -> 1.53 us
    pallas_call x1, Pallas kernels: 41.5 us -> 37.6 us  [on_device(): pl.pallas_call(kernel, out_shape=(OUT_TYPE(coupling.shape, F32), jax.Shap...]
    unnamed x4, local copies, waits for them, and re-layouts: 2.88 us -> 1.53 us
where the time goes in v2:
time: 39.9 us; the launch traced here: 39.7 us
  Pallas kernels  37.6 us (94%)
  local copies, waits for them, and re-layouts  1.53 us (4%)
  between operations  0.65 us (2%)
    pallas_call x1, Pallas kernels, on_device(): pl.pallas_call(kernel, out_shape=(OUT_TYPE(coupling.shape, F32), jax.Shap...  37.6 us
    unnamed x4, local copies, waits for them, and re-layouts  1.53 us

profile of v2, /device:TPU:0, one launch (start us, length us, event | category | flops | bytes accessed | tf_op | source)
XLA Modules:
  0.0 39.7 jit_solution(3763957712612835732)
XLA Ops:
  0.6 37.6 %shard_map.77 = (f32[2,1,384,384]{3,2,1,0:T(8,128)S(1)}, f32[4]{0:T(128)}) custom-call(f32[2,1,384,384]{3,2,1,0:T(8,128)} %coupling_hbm.1, f32[2,1,384,384]{3,2,1,0:T(8,128)} %schur_hbm.1, s32[2,1,2048]{2,1,0:T(1,128)} %rows_hbm.1, s32[2,1,2048]{2,1,0:T(1,128)} %shift_hbm.1, s32[2,1,2048]{2,1,0:T(1,128)} %hyper_hbm.1, f32[2,1,2048]{2,1,0:T(1,128)} %values_hbm.1), custom_call_target="tpu_custom_call" | custom-call | tf_op jit(solution)/shard_map/pallas_call | solution.py:449
  38.2 0.0 copy-start
  38.2 1.0 %copy.10 = f32[2,1,384,384]{3,2,1,0:T(8,128)} copy(f32[2,1,384,384]{3,2,1,0:T(8,128)S(1)} %get-tuple-element.2) | data formatting | bytes 2359296
  39.2 0.0 copy-done
  39.2 0.5 %copy.11 = f32[4]{0:T(128)} copy(f32[4]{0:T(128)S(1)} %copy-done) | data formatting | bytes 32
Async XLA Ops:
  38.2 1.0 %copy-start = (f32[4]{0:T(128)S(1)}, f32[4]{0:T(128)}, u32[]{:S(2)}) copy-start(f32[4]{0:T(128)} %get-tuple-element.7) | copy-start | bytes 52

commit v3 on v2

--- a/solution.py
+++ b/solution.py
@@ -60,6 +60,7 @@
     in_b,
     in_c,
     weights,
+    adjoint,
     partials,
     load_sem,
     entry_sem,
@@ -78,6 +79,7 @@
     rank = me * spaces + mine
     is_last = me == devices - 1
     staggered = spaces % 2 == 0 and spaces > 1
+    early = devices > 1 and steps <= 2
     goes_first = lax.rem(mine, 2) == 0 if staggered else mine >= 0
 
     def peer(k):
@@ -311,41 +313,6 @@
         sums = lax.dot_general(spread, onehot, NT, preferred_element_type=F32)
         weights[p] = sums[:padded] + sums[padded : 2 * padded] + sums[2 * padded :]
 
-    if devices > 1:
-
-        @pl.when(jnp.logical_not(is_last))
-        def _():
-            for i in range(blocks):
-                hop(i).wait_recv()
-                unpack(i)
-                if i == 1:
-                    first_half(c_hi, c_lo, 0)
-                if i > 0:
-                    first_half(c_hi, c_lo, i)
-            for i in range(blocks):
-                right = slice(i * TILE, order)
-                fresh = second_half(c_hi, c_lo, result.at[0], i)
-                result[0, band(i), right] = fresh
-
-                @pl.when(me > 0)
-                def _():
-                    pack(i, result.at[0])
-                    hop(i).start()
-
-            for p in range(steps - 1, 0, -1):
-                for i in range(blocks):
-                    first_half(g_hi.at[p], g_lo.at[p], i)
-                for i in range(blocks):
-                    result[p, band(i), i * TILE :] = second_half(
-                        g_hi.at[p], g_lo.at[p], s_in.at[p], i
-                    )
-                mirror(result.at[p])
-                if p > 1:
-                    set_current(result[p])
-
-    if steps > 1 or devices > 1:
-        mirror(result.at[0])
-
     def diagonals(p):
         pieces = []
         for b in range(blocks):
@@ -367,17 +334,18 @@
             pieces.append(lines)
         return pieces
 
-    total = jnp.zeros((8, TILE), F32)
-    group_of = lax.broadcasted_iota(jnp.int32, (padded, TILE), 0) // NHYP
-    for p in range(steps):
-        for b, lines in enumerate(diagonals(p)):
-            matched = jnp.zeros((padded, TILE), F32)
-            for d in range(2 * REACH + 1):
-                matched = jnp.where(group_of == d, lines[d], matched)
-            terms = matched * weights[p, :, band(b)]
-            for k in range(padded // 8):
-                total = total + terms[8 * k : 8 * (k + 1)]
-    partials[rank] = total
+    def direct_terms():
+        total = jnp.zeros((8, TILE), F32)
+        group_of = lax.broadcasted_iota(jnp.int32, (padded, TILE), 0) // NHYP
+        for p in range(steps):
+            for b, lines in enumerate(diagonals(p)):
+                matched = jnp.zeros((padded, TILE), F32)
+                for d in range(2 * REACH + 1):
+                    matched = jnp.where(group_of == d, lines[d], matched)
+                terms = matched * weights[p, :, band(b)]
+                for k in range(padded // 8):
+                    total = total + terms[8 * k : 8 * (k + 1)]
+        return total
 
     def exchange(k):
         other, where = peer(k)
@@ -394,7 +362,97 @@
         exchange(k).start()
         return carry
 
-    lax.fori_loop(1, group, start_exchange, 0)
+    def prepare():
+        mirror(result.at[0])
+        partials[rank] = direct_terms()
+        down = lax.broadcasted_iota(jnp.int32, (order, order), 0)
+        offset = down - lax.broadcasted_iota(jnp.int32, (order, order), 1)
+
+        def for_hyper(k, carry):
+            for p in range(steps):
+                gains = (c_hi[...], c_lo[...]) if p == 0 else (g_hi[p], g_lo[p])
+                spots = jnp.zeros((order, order), F32)
+                for d in range(-REACH, REACH + 1):
+                    line = weights[p, pl.ds((d + REACH) * NHYP + k, 1), :]
+                    here = offset == d
+                    if d != 0:
+                        here = jnp.logical_or(here, offset == (d - order if d > 0 else d + order))
+                    spots = jnp.where(here, line, spots)
+                right = product(split(spots), gains, NN)
+                both = product(split(right.T), gains, NN)
+                adjoint[k] = both if p == 0 else adjoint[k] + both
+            return carry
+
+        lax.fori_loop(0, NHYP, for_hyper, 0)
+
+    def finish_early():
+        total = partials[rank]
+        spot = lax.broadcasted_iota(jnp.int32, (8, TILE), 0)
+        current = b_hi[...].astype(F32) + b_lo[...].astype(F32)
+        for k in range(NHYP):
+            line = jnp.sum(adjoint[k] * current, axis=0, keepdims=True)
+            line = sum(line[:, band(i)] for i in range(blocks))
+            total = total + jnp.where(spot == k, line, 0.0)
+        partials[rank] = total
+        lax.fori_loop(1, group, start_exchange, 0)
+
+    if early:
+
+        @pl.when(me == 0)
+        def _():
+            prepare()
+
+    if devices > 1:
+
+        @pl.when(jnp.logical_not(is_last))
+        def _():
+            for i in range(blocks):
+                hop(i).wait_recv()
+                unpack(i)
+                if i == 1:
+                    first_half(c_hi, c_lo, 0)
+                if i > 0 and not (early and i == blocks - 1):
+                    first_half(c_hi, c_lo, i)
+            if early:
+
+                @pl.when(me == 0)
+                def _():
+                    finish_early()
+
+                first_half(c_hi, c_lo, blocks - 1)
+            for i in range(blocks):
+                right = slice(i * TILE, order)
+                fresh = second_half(c_hi, c_lo, result.at[0], i)
+                result[0, band(i), right] = fresh
+
+                @pl.when(me > 0)
+                def _():
+                    pack(i, result.at[0])
+                    hop(i).start()
+
+            for p in range(steps - 1, 0, -1):
+                for i in range(blocks):
+                    first_half(g_hi.at[p], g_lo.at[p], i)
+                for i in range(blocks):
+                    result[p, band(i), i * TILE :] = second_half(
+                        g_hi.at[p], g_lo.at[p], s_in.at[p], i
+                    )
+                mirror(result.at[p])
+                if p > 1:
+                    set_current(result[p])
+
+    if steps > 1 or devices > 1:
+        mirror(result.at[0])
+
+    if early:
+
+        @pl.when(me != 0)
+        def _():
+            partials[rank] = direct_terms()
+            lax.fori_loop(1, group, start_exchange, 0)
+    else:
+        partials[rank] = direct_terms()
+        lax.fori_loop(1, group, start_exchange, 0)
 
     def take(k, carry):
         other, where = peer(k)
@@ -469,6 +527,7 @@
             *travelling,
             *travelling,
             pltpu.VMEM((steps, padded, order), F32),
+            pltpu.VMEM((NHYP, order, order), F32),
             pltpu.VMEM((group, 8, TILE), F32),
             pltpu.SemaphoreType.DMA((2, steps)),
             pltpu.SemaphoreType.DMA((len(entries),)),

time: 39.9 us -> 37.6 us (0.942); the launches traced: 39.7 us -> 37 us
  Pallas kernels: 37.6 us -> 34.8 us
    pallas_call x1, Pallas kernels: 37.6 us -> 34.8 us  [on_device(): pl.pallas_call(kernel, out_shape=(OUT_TYPE(coupling.shape, F32), jax.Shap...]
where the time goes in v3:
time: 37.6 us; the launch traced here: 37 us
  Pallas kernels  34.8 us (93%)
  local copies, waits for them, and re-layouts  1.53 us (4%)
  between operations  0.65 us (2%)
    pallas_call x1, Pallas kernels, on_device(): pl.pallas_call(kernel, out_shape=(OUT_TYPE(coupling.shape, F32), jax.Shap...  34.8 us
    unnamed x4, local copies, waits for them, and re-layouts  1.53 us

profile of v3, /device:TPU:0, one launch (start us, length us, event | category | flops | bytes accessed | tf_op | source)
XLA Modules:
  0.0 37.0 jit_solution(11378618902665210518)
XLA Ops:
  0.6 34.8 %shard_map.77 = (f32[2,1,384,384]{3,2,1,0:T(8,128)S(1)}, f32[4]{0:T(128)}) custom-call(f32[2,1,384,384]{3,2,1,0:T(8,128)} %coupling_hbm.1, f32[2,1,384,384]{3,2,1,0:T(8,128)} %schur_hbm.1, s32[2,1,2048]{2,1,0:T(1,128)} %rows_hbm.1, s32[2,1,2048]{2,1,0:T(1,128)} %shift_hbm.1, s32[2,1,2048]{2,1,0:T(1,128)} %hyper_hbm.1, f32[2,1,2048]{2,1,0:T(1,128)} %values_hbm.1), custom_call_target="tpu_custom_call" | custom-call | tf_op jit(solution)/shard_map/pallas_call | solution.py:507
  35.5 0.0 copy-start
  35.5 1.0 %copy.10 = f32[2,1,384,384]{3,2,1,0:T(8,128)} copy(f32[2,1,384,384]{3,2,1,0:T(8,128)S(1)} %get-tuple-element.2) | data formatting | bytes 2359296
  36.5 0.0 copy-done
  36.5 0.5 %copy.11 = f32[4]{0:T(128)} copy(f32[4]{0:T(128)S(1)} %copy-done) | data formatting | bytes 32
Async XLA Ops:
  35.5 1.0 %copy-start = (f32[4]{0:T(128)S(1)}, f32[4]{0:T(128)}, u32[]{:S(2)}) copy-start(f32[4]{0:T(128)} %get-tuple-element.7) | copy-start | bytes 52

commit v4 on v3

--- a/solution.py
+++ b/solution.py
@@ -266,7 +266,7 @@
         @pl.when(jnp.logical_and(is_last, goes_first))
         def _():
             for i in range(blocks):
-                if staggered and i == blocks - 1:
+                if staggered and i == 1:
                     pl.semaphore_signal(
                         turn_sem, inc=1, device_id={"space": mine + 1}, device_id_type=MESH
                     )

time: 37.6 us -> 38.9 us (1.035)
  Pallas kernels: 34.8 us -> 36.1 us
    pallas_call x1, Pallas kernels: 34.8 us -> 36.1 us  [on_device(): pl.pallas_call(kernel, out_shape=(OUT_TYPE(coupling.shape, F32), jax.Shap...]
where the time goes in v4:
time: 38.9 us; the launch traced here: 38.3 us
  Pallas kernels  36.1 us (93%)
  local copies, waits for them, and re-layouts  1.53 us (4%)
  between operations  0.65 us (2%)
    pallas_call x1, Pallas kernels, on_device(): pl.pallas_call(kernel, out_shape=(OUT_TYPE(coupling.shape, F32), jax.Shap...  36.1 us
    unnamed x4, local copies, waits for them, and re-layouts  1.53 us

profile of v4, /device:TPU:0, one launch (start us, length us, event | category | flops | bytes accessed | tf_op | source)
XLA Modules:
  0.0 38.3 jit_solution(11034959365582035197)
XLA Ops:
  0.6 36.1 %shard_map.77 = (f32[2,1,384,384]{3,2,1,0:T(8,128)S(1)}, f32[4]{0:T(128)}) custom-call(f32[2,1,384,384]{3,2,1,0:T(8,128)} %coupling_hbm.1, f32[2,1,384,384]{3,2,1,0:T(8,128)} %schur_hbm.1, s32[2,1,2048]{2,1,0:T(1,128)} %rows_hbm.1, s32[2,1,2048]{2,1,0:T(1,128)} %shift_hbm.1, s32[2,1,2048]{2,1,0:T(1,128)} %hyper_hbm.1, f32[2,1,2048]{2,1,0:T(1,128)} %values_hbm.1), custom_call_target="tpu_custom_call" | custom-call | tf_op jit(solution)/shard_map/pallas_call | solution.py:507
  36.8 0.0 copy-start
  36.8 1.0 %copy.10 = f32[2,1,384,384]{3,2,1,0:T(8,128)} copy(f32[2,1,384,384]{3,2,1,0:T(8,128)S(1)} %get-tuple-element.2) | data formatting | bytes 2359296
  37.8 0.0 copy-done
  37.8 0.5 %copy.11 = f32[4]{0:T(128)} copy(f32[4]{0:T(128)S(1)} %copy-done) | data formatting | bytes 32
Async XLA Ops:
  36.8 1.0 %copy-start = (f32[4]{0:T(128)S(1)}, f32[4]{0:T(128)}, u32[]{:S(2)}) copy-start(f32[4]{0:T(128)} %get-tuple-element.7) | copy-start | bytes 52
